TPU v7x, 32 devices: a whole 2x2x4 slice. The times are simulated.
32 devices in a mesh: clip: 2 (over x), tm: 4 (over z), chan: 4 (over y, core).
Axes of the slice: x: 2, y: 2, z: 4, core: 2. Of those that a mesh axis runs over, the one named last changes fastest.
Arguments:
- signal: bfloat16 [2, 4096, 256], P('clip', 'tm', 'chan'), may hold values from -6 to 6
- conv_first: bfloat16 [3, 256, 128], P(None, 'chan'), may hold values from -0.21875 to 0.21875
- conv_second: bfloat16 [128, 256], P(None, 'chan'), may hold values from -0.5 to 0.5
- conv_down: bfloat16 [16, 256, 512], P(None, 'chan'), may hold values from -0.09375 to 0.09375
- cotangent: bfloat16 [2, 512, 512], P('clip', 'tm'), may hold values from -6 to 6
Outputs:
- grad_signal: bfloat16 [2, 4096, 256], P('clip', 'tm', 'chan')
- grad_first: float32 [3, 256, 128], P(None, 'chan')
- grad_second: float32 [128, 256], P(None, 'chan')
- grad_down: float32 [16, 256, 512], P(None, 'chan')
All inputs are finite; a program needn't handle non-finite values.
Results may differ from a plain program's by a relative error of at most 0.018.
Values may be sent and summed in bfloat16 or wider, within the bound.
No kernel may reach another device: no remote copies, remote signals or barrier semaphores. Data moves between devices by JAX's collectives and lax.ppermute only.
A program may use at most 64 MiB of HBM per device.

v0:
```python
import jax
import jax.numpy as jnp
from jax import lax
from jax.sharding import PartitionSpec as P

KRES = 3
STRIDE = 8
RIM = 10


def shifted(block, axis, distance):
    devices = range(lax.axis_size(axis))
    route = [(i - distance, i) for i in devices if i - distance in devices]
    return lax.ppermute(block, axis, route)


def elu(value):
    return jnp.where(value > 0, value, jnp.exp(jnp.minimum(value, 0.0)) - 1.0)


def slope(value):
    return jnp.where(value > 0, 1.0, jnp.exp(jnp.minimum(value, 0.0)))


def contract_rows(left, right):
    return lax.dot_general(
        left, right, (((0,), (0,)), ((), ())), preferred_element_type=jnp.float32
    )


def contract_cols(left, right):
    return lax.dot_general(
        left, right, (((1,), (1,)), ((), ())), preferred_element_type=jnp.float32
    )


def causal_conv(values, weights, span):
    total = jnp.zeros((span, weights.shape[2]), jnp.float32)
    for k in range(KRES):
        total = total + jnp.dot(
            values[k : k + span], weights[k], preferred_element_type=jnp.float32
        )
    return total


def on_device(signal, conv_first, conv_second, conv_down, cotangent):
    frames = signal[0]
    length, local_ch = frames.shape
    span = length + RIM - KRES + 1
    borrowed = shifted(frames[length - RIM :], "tm", 1)
    padded = jnp.concatenate([borrowed, frames], axis=0)
    act = elu(padded.astype(jnp.float32)).astype(jnp.bfloat16)
    hidden = lax.psum(causal_conv(act, conv_first, span).astype(jnp.bfloat16), "chan").astype(
        jnp.float32
    )
    inner = elu(hidden).astype(jnp.bfloat16)
    resid = padded[KRES - 1 :].astype(jnp.float32) + jnp.dot(
        inner, conv_second, preferred_element_type=jnp.float32
    )
    feed = elu(resid).astype(jnp.bfloat16)
    blocks = feed.reshape(span // STRIDE, STRIDE * local_ch)
    wide = conv_down.reshape(2, STRIDE * local_ch, conv_down.shape[2])
    upstream = cotangent[0]
    count = upstream.shape[0]
    front = contract_cols(upstream, wide[0])
    back = contract_cols(upstream, wide[1])
    dblocks = jnp.pad(front, ((0, 1), (0, 0))) + jnp.pad(back, ((1, 0), (0, 0)))
    down_raw = jnp.stack(
        [contract_rows(blocks[:count], upstream), contract_rows(blocks[1:], upstream)]
    )
    down_raw = down_raw.reshape(conv_down.shape)
    dresid = dblocks.reshape(span, local_ch) * slope(resid)
    dres16 = dresid.astype(jnp.bfloat16)
    second_raw = contract_rows(inner, dres16)
    dinner = lax.psum(contract_cols(dres16, conv_second).astype(jnp.bfloat16), "chan").astype(
        jnp.float32
    )
    dhid = (dinner * slope(hidden)).astype(jnp.bfloat16)
    first_raw = jnp.stack([contract_rows(act[k : k + span], dhid) for k in range(KRES)])
    dact = jnp.zeros(padded.shape, jnp.float32)
    for k in range(KRES):
        dact = dact + jnp.pad(contract_cols(dhid, conv_first[k]), ((k, KRES - 1 - k), (0, 0)))
    dpadded = dact * slope(padded.astype(jnp.float32)) + jnp.pad(dresid, ((KRES - 1, 0), (0, 0)))
    returned = shifted(dpadded[:RIM], "tm", -1)
    grad_frames = dpadded[RIM:] + jnp.pad(returned, ((length - RIM, 0), (0, 0)))
    first_total, second_total, down_total = lax.psum(
        (first_raw, second_raw, down_raw), ("clip", "tm")
    )
    factor = 1.0 / jnp.sqrt(
        jnp.float32(lax.axis_size("clip") * lax.axis_size("tm") * (length // STRIDE))
    )
    return (
        grad_frames.astype(jnp.bfloat16)[None],
        first_total * factor,
        second_total * factor,
        down_total * factor,
    )


def solution(mesh):
    return jax.shard_map(
        on_device,
        mesh=mesh,
        in_specs=(
            P("clip", "tm", "chan"),
            P(None, "chan", None),
            P(None, "chan"),
            P(None, "chan", None),
            P("clip", "tm", None),
        ),
        out_specs=(
            P("clip", "tm", "chan"),
            P(None, "chan", None),
            P(None, "chan"),
            P(None, "chan", None),
        ),
        check_vma=False,
    )
```

profile of v0, /device:TPU:0, one launch (start us, length us, event | category | flops | bytes accessed | tf_op | source)
XLA Modules:
  0.0 208.7 jit_solution(13187131113075802272)
XLA Ops:
  7.2 0.0 copy-start
  7.2 0.0 copy-start.1
  7.2 0.0 copy-start.3
  7.2 0.0 all-reduce.12.cloned.1.call-start
  7.2 0.9 slice_bitcast_fusion
  8.1 4.9 %collective-permute-start = (bf16[10,64]{0,1:T(8,128)(2,1)S(1)}, bf16[10,64]{0,1:T(8,128)(2,1)S(1)}, u32[]{:S(2)}, u32[]{:S(2)}) collective-permute-start(bf16[10,64]{0,1:T(8,128)(2,1)S(1)} %slice_bitcast_fusion), channel_id=1, source_target_pairs={{0,4},{4,8},{8,12},{1,5},{5,9},{9,13},{2,6},{6,10},{10,14},{3,7},{... | collective-permute-start | bytes 3848 | tf_op jit(solution)/shard_map/ppermute | solution.py:14
  13.0 1.3 fusion.56
  14.3 0.0 copy-done
  14.3 0.3 fusion.22
  14.7 0.0 collective-permute-done
  14.7 0.0 copy-done.1
  14.7 0.1 fusion.14
  14.8 0.0 copy-done.3
  14.8 0.3 fusion.29
  15.2 0.5 convolution_add_fusion.1
  15.6 0.0 copy-start.4
  15.6 1.2 fusion
  16.8 0.0 all-reduce.12.cloned.1.call-update
  16.8 0.0 all-reduce.14.cloned.1.call-start
  16.9 0.3 fusion.20
  17.2 0.1 reshape.23
  17.4 0.2 copy.10
  17.6 32.4 %all-reduce.12.cloned.1.call-done = bf16[1032,128]{1,0:T(8,128)(2,1)} async-done(((bf16[1032,128]{1,0:T(8,128)(2,1)}), bf16[1032,128]{1,0:T(8,128)(2,1)}) %all-reduce.12.cloned.1.call-update) | async-done | bytes 264208 | tf_op jit(solution)/shard_map/psum | solution.py:53
  50.0 0.0 copy-done.4
  50.0 1.3 fusion.9
  51.3 0.1 fusion.57
  51.4 0.2 copy.11
  51.6 0.2 slice.73
  51.8 0.2 copy.12
  52.0 0.2 slice.75
  52.2 1.0 convolution_convert_fusion
  53.2 0.0 all-reduce.14.cloned.1.call-update
  53.3 0.0 all-reduce.16.cloned.1.call-start
  53.3 0.3 convolution_bitcast_fusion
  53.6 0.3 convolution_bitcast_fusion.1
  53.9 0.0 copy-start.2
  54.0 1.5 pad_maximum_fusion
  55.4 30.2 %all-reduce.14.cloned.1.call-done = bf16[1032,128]{1,0:T(8,128)(2,1)} async-done(((bf16[1032,128]{1,0:T(8,128)(2,1)}), bf16[1032,128]{1,0:T(8,128)(2,1)}) %all-reduce.14.cloned.1.call-update) | async-done | bytes 264208 | tf_op jit(solution)/shard_map/psum | solution.py:75
  85.6 0.0 copy-done.2
  85.6 1.1 fusion.3
  86.7 0.2 convolution_bitcast_fusion.2
  87.0 0.2 convolution_bitcast_fusion.3
  87.2 0.2 convolution_bitcast_fusion.4
  87.4 0.7 pad_maximum_fusion.2
  88.1 0.0 all-reduce.16.cloned.1.call-update
  88.1 0.3 fusion.31
  88.4 39.2 %psum.38 = f32[128,64]{0,1:T(8,128)S(1)} all-reduce(f32[128,64]{0,1:T(8,128)S(1)} %fusion.31), channel_id=1, replica_groups=mesh['clip'=2,'tm'=4,'chan'=4] {'clip','tm'}, use_global_device_ids=true, to_apply=%region_3.4 | all-reduce | flops 8192 | bytes 65536 | tf_op jit(solution)/shard_map/psum | solution.py:86
  127.6 0.2 fusion.37
  127.8 0.2 fusion.40
  128.0 0.2 fusion.43
  128.2 0.3 fusion.11
  128.6 1.3 collective-permute-start.1
  129.9 0.6 broadcast_multiply_fusion.2
  130.5 3.9 %collective-permute-done.1 = f32[10,64]{0,1:T(8,128)S(1)} collective-permute-done((f32[10,64]{0,1:T(8,128)S(1)}, f32[10,64]{0,1:T(8,128)S(1)}, u32[]{:S(2)}, u32[]{:S(2)}) %collective-permute-start.1) | collective-permute-done | bytes 2592 | tf_op jit(solution)/shard_map/ppermute | solution.py:14
  134.4 0.8 fusion.17
  135.2 62.3 %all-reduce.16.cloned.1.call-done = (f32[3,64,128]{2,1,0:T(8,128)}, f32[16,64,512]{2,1,0:T(8,128)}) async-done(((f32[3,64,128]{2,1,0:T(8,128)}, f32[16,64,512]{2,1,0:T(8,128)}), (f32[3,64,128]{2,1,0:T(8,128)}, f32[16,64,512]{2,1,0:T(8,128)})) %all-reduce.16.cloned.1.call-update) | async-done | bytes 2195472 | tf_op jit(solution)/shard_map/psum | solution.py:86
  197.5 1.5 broadcast_multiply_fusion.1
  199.0 3.2 %broadcast_multiply_fusion = f32[16,64,512]{2,1,0:T(8,128)} fusion(f32[16,64,512]{2,1,0:T(8,128)} %get-tuple-element.5), kind=kLoop, calls=%fused_computation.10 | loop fusion | flops 524288 | bytes 4194304 | tf_op jit(solution)/shard_map/mul | solution.py:96
  (2 shorter events, 0.1 us)
Async XLA Ops:
  7.2 7.2 %copy-start = (bf16[1,128,512]{2,1,0:T(8,128)(2,1)S(1)}, bf16[1,128,512]{2,1,0:T(8,128)(2,1)}, u32[]{:S(2)}) copy-start(bf16[1,128,512]{2,1,0:T(8,128)(2,1)} %param.9) | copy-start | bytes 393220
  7.2 7.5 %copy-start.1 = (bf16[1,1024,64]{1,2,0:T(8,128)(2,1)S(1)}, bf16[1,1024,64]{1,2,0:T(8,128)(2,1)}, u32[]{:S(2)}) copy-start(bf16[1,1024,64]{1,2,0:T(8,128)(2,1)} %param.5) | copy-start | bytes 393220
  7.2 7.6 %copy-start.3 = (bf16[3,64,128]{2,1,0:T(8,128)(2,1)S(1)}, bf16[3,64,128]{2,1,0:T(8,128)(2,1)}, u32[]{:S(2)}) copy-start(bf16[3,64,128]{2,1,0:T(8,128)(2,1)} %param.6) | copy-start | bytes 147460
  7.2 42.8 %all-reduce.12.cloned.1.call-start = ((), (), s32[]{:S(2)}) async-start(), calls=%async_computation | async-start | bytes 528384 | tf_op jit(solution)/shard_map/psum | solution.py:53
  8.1 6.5 %collective-permute-start = (bf16[10,64]{0,1:T(8,128)(2,1)S(1)}, bf16[10,64]{0,1:T(8,128)(2,1)S(1)}, u32[]{:S(2)}, u32[]{:S(2)}) collective-permute-start(bf16[10,64]{0,1:T(8,128)(2,1)S(1)} %slice_bitcast_fusion), channel_id=1, source_target_pairs={{0,4},{4,8},{8,12},{1,5},{5,9},{9,13},{2,6},{6,10},{10,14},{3,7},{... | collective-permute-start | bytes 3848 | tf_op jit(solution)/shard_map/ppermute | solution.py:14
  15.6 34.4 %copy-start.4 = (bf16[128,64]{0,1:T(8,128)(2,1)S(1)}, bf16[128,64]{0,1:T(8,128)(2,1)}, u32[]{:S(2)}) copy-start(bf16[128,64]{0,1:T(8,128)(2,1)} %param.7) | copy-start | bytes 49156
  16.8 68.8 %all-reduce.14.cloned.1.call-start = ((), (), s32[]{:S(2)}) async-start(), calls=%async_computation.1 | async-start | bytes 528384 | tf_op jit(solution)/shard_map/psum | solution.py:75
  53.3 144.2 %all-reduce.16.cloned.1.call-start = ((), (), s32[]{:S(2)}) async-start(), calls=%async_computation.2 | async-start | bytes 4390912 | tf_op jit(solution)/shard_map/psum | solution.py:86
  53.9 31.7 %copy-start.2 = (bf16[1032,128]{1,0:T(8,128)(2,1)S(1)}, bf16[1032,128]{1,0:T(8,128)(2,1)}, u32[]{:S(2)}) copy-start(bf16[1032,128]{1,0:T(8,128)(2,1)} %all-reduce.12.cloned.1.call-done) | copy-start | bytes 792580
  128.6 5.8 %collective-permute-start.1 = (f32[10,64]{0,1:T(8,128)S(1)}, f32[10,64]{0,1:T(8,128)S(1)}, u32[]{:S(2)}, u32[]{:S(2)}) collective-permute-start(f32[10,64]{0,1:T(8,128)S(1)} %slice.82), channel_id=1, source_target_pairs={{4,0},{8,4},{12,8},{5,1},{9,5},{13,9},{6,2},{10,6},{14,10},{7,3},{... | collective-permute-start | bytes 7688 | tf_op jit(solution)/shard_map/ppermute | solution.py:14
Sparse Core Ops, SparseCore 0:
  16.9 32.9 all-reduce.11
  53.4 32.2 all-reduce.13
  90.0 107.4 all-reduce.15
where the time goes:
time: 209 us
  waiting for transfers between devices  129 us (62%)
  blocking collectives  39.2 us (19%)
  between operations  13.9 us (7%)
  other arithmetic  9.89 us (5%)
  matrix products  7.15 us (3%)
  starting transfers between devices  6.33 us (3%)
  local copies, waits for them, and re-layouts  3.4 us (2%)
    psum x1, waiting for transfers between devices, on_device(): lax.psum((first_raw, second_raw, down_raw), ('clip', 'tm'))  62.3 us
    psum x1, blocking collectives, on_device(): lax.psum((first_raw, second_raw, down_raw), ('clip', 'tm'))  39.2 us
    psum x1, waiting for transfers between devices, on_device(): lax.psum(causal_conv(act, conv_first, span).astype(jnp.bfloat16), 'chan')  32.4 us
    psum x1, waiting for transfers between devices, on_device(): lax.psum(contract_cols(dres16, conv_second).astype(jnp.bfloat16), 'chan')  30.2 us
    ppermute x2, starting transfers between devices, shifted(): return lax.ppermute(block, axis, route)  6.21 us
  transfers between devices with their start and end apart: 5, of which 4 were waited for; matrix products, arithmetic and copies ran while one was open for 3% of the time, Pallas kernels for 0%

commit v1 on v0

--- a/solution.py
+++ b/solution.py
@@ -50,9 +50,9 @@
     borrowed = shifted(frames[length - RIM :], "tm", 1)
     padded = jnp.concatenate([borrowed, frames], axis=0)
     act = elu(padded.astype(jnp.float32)).astype(jnp.bfloat16)
-    hidden = lax.psum(causal_conv(act, conv_first, span).astype(jnp.bfloat16), "chan").astype(
-        jnp.float32
-    )
+    hidden = jnp.sum(
+        lax.all_gather(causal_conv(act, conv_first, span).astype(jnp.bfloat16), "chan"), axis=0
+    ).astype(jnp.float32)
     inner = elu(hidden).astype(jnp.bfloat16)
     resid = padded[KRES - 1 :].astype(jnp.float32) + jnp.dot(
         inner, conv_second, preferred_element_type=jnp.float32

time: 209 us -> 197 us (0.943)
  waiting for transfers between devices: 129 us -> 115 us
  other arithmetic: 9.89 us -> 12.3 us
    psum x1 -> x0, waiting for transfers between devices: 32.4 us -> none  [on_device(): lax.psum(causal_conv(act, conv_first, span).astype(jnp.bfloat16), 'chan')]
    all_gather x0 -> x1, waiting for transfers between devices: none -> 17.7 us  [on_device(): lax.all_gather(causal_conv(act, conv_first, span).astype(jnp.bfloat16), '...]
  transfers between devices with their start and end apart: 5 -> 5, of which waited for: 4 -> 5; matrix products, arithmetic and copies ran while one was open for 3% -> 3% of each run, Pallas kernels for 0% -> 0%
where the time goes in v1:
time: 197 us; the launch traced here: 196 us
  waiting for transfers between devices  115 us (58%)
  blocking collectives  39.2 us (20%)
  between operations  14 us (7%)
  other arithmetic  12.3 us (6%)
  matrix products  7.67 us (4%)
  starting transfers between devices  6.33 us (3%)
  local copies, waits for them, and re-layouts  2.24 us (1%)
    psum x1, waiting for transfers between devices, on_device(): lax.psum((first_raw, second_raw, down_raw), ('clip', 'tm'))  62.3 us
    psum x1, blocking collectives, on_device(): lax.psum((first_raw, second_raw, down_raw), ('clip', 'tm'))  39.2 us
    psum x1, waiting for transfers between devices, on_device(): lax.psum(contract_cols(dres16, conv_second).astype(jnp.bfloat16), 'chan')  29.2 us
    all_gather x1, waiting for transfers between devices, on_device(): lax.all_gather(causal_conv(act, conv_first, span).astype(jnp.bfloat16), '...  17.7 us
    ppermute x2, starting transfers between devices, shifted(): return lax.ppermute(block, axis, route)  6.21 us
    ppermute x2, waiting for transfers between devices, shifted(): return lax.ppermute(block, axis, route)  5.31 us
  transfers between devices with their start and end apart: 5, of which 5 were waited for; matrix products, arithmetic and copies ran while one was open for 3% of the time, Pallas kernels for 0%

profile of v1, /device:TPU:0, one launch (start us, length us, event | category | flops | bytes accessed | tf_op | source)
XLA Modules:
  0.0 196.2 jit_solution(17689625439678861433)
XLA Ops:
  7.2 0.0 copy-start
  7.2 0.0 copy-start.3
  7.2 0.0 copy-start.1
  7.2 0.0 all-gather.3.cloned.1.call-start
  7.2 0.9 slice_bitcast_fusion
  8.1 4.9 %collective-permute-start = (bf16[10,64]{0,1:T(8,128)(2,1)S(1)}, bf16[10,64]{0,1:T(8,128)(2,1)S(1)}, u32[]{:S(2)}, u32[]{:S(2)}) collective-permute-start(bf16[10,64]{0,1:T(8,128)(2,1)S(1)} %slice_bitcast_fusion), channel_id=1, source_target_pairs={{0,4},{4,8},{8,12},{1,5},{5,9},{9,13},{2,6},{6,10},{10,14},{3,7},{... | collective-permute-start | bytes 3848 | tf_op jit(solution)/shard_map/ppermute | solution.py:14
  13.1 1.4 collective-permute-done
  14.5 1.1 fusion.14
  15.5 1.1 fusion.29
  16.6 1.2 convolution_add_fusion.1
  17.8 0.0 copy-done.3
  17.8 1.2 fusion
  19.0 0.0 all-gather.3.cloned.1.call-update
  19.0 0.0 all-reduce.11.cloned.1.call-start
  19.0 0.0 copy-done.1
  19.0 0.1 fusion.56
  19.1 0.0 copy-done
  19.2 0.3 fusion.22
  19.5 0.3 fusion.20
  19.8 0.0 copy-start.2
  19.8 0.0 copy-start.4
  19.8 0.1 reshape.23
  20.0 0.2 copy.10
  20.2 17.7 %all-gather.3.cloned.1.call-done = bf16[4128,128]{1,0:T(8,128)(2,1)} async-done(((bf16[1032,128]{1,0:T(8,128)(2,1)}), bf16[4128,128]{1,0:T(8,128)(2,1)}) %all-gather.3.cloned.1.call-update) | async-done | bytes 1056784 | tf_op jit(solution)/shard_map/all_gather | solution.py:54
  37.9 1.5 reduce_sum.12
  39.4 0.0 copy-done.2
  39.4 0.0 copy-done.4
  39.4 0.4 fusion.9
  39.8 0.1 fusion.57
  39.9 0.2 copy.11
  40.0 0.2 slice.73
  40.3 0.2 copy.12
  40.4 0.2 slice.75
  40.7 1.0 convolution_convert_fusion
  41.7 0.0 all-reduce.11.cloned.1.call-update
  41.7 0.0 all-reduce.13.cloned.1.call-start
  41.8 0.3 convolution_bitcast_fusion
  42.1 0.3 convolution_bitcast_fusion.1
  42.4 1.5 pad_maximum_fusion
  43.9 29.2 %all-reduce.11.cloned.1.call-done = bf16[1032,128]{1,0:T(8,128)(2,1)} async-done(((bf16[1032,128]{1,0:T(8,128)(2,1)}), bf16[1032,128]{1,0:T(8,128)(2,1)}) %all-reduce.11.cloned.1.call-update) | async-done | bytes 264208 | tf_op jit(solution)/shard_map/psum | solution.py:75
  73.1 1.1 fusion.3
  74.2 0.2 convolution_bitcast_fusion.2
  74.5 0.2 convolution_bitcast_fusion.3
  74.7 0.2 convolution_bitcast_fusion.4
  74.9 0.7 pad_maximum_fusion.2
  75.6 0.0 all-reduce.13.cloned.1.call-update
  75.6 0.3 fusion.31
  75.9 39.2 %psum.30 = f32[128,64]{0,1:T(8,128)S(1)} all-reduce(f32[128,64]{0,1:T(8,128)S(1)} %fusion.31), channel_id=1, replica_groups=mesh['clip'=2,'tm'=4,'chan'=4] {'clip','tm'}, use_global_device_ids=true, to_apply=%region_3.4 | all-reduce | flops 8192 | bytes 65536 | tf_op jit(solution)/shard_map/psum | solution.py:86
  115.1 0.2 fusion.37
  115.3 0.2 fusion.40
  115.5 0.2 fusion.43
  115.8 0.3 fusion.11
  116.1 1.3 collective-permute-start.1
  117.4 0.6 broadcast_multiply_fusion.2
  118.0 3.9 %collective-permute-done.1 = f32[10,64]{0,1:T(8,128)S(1)} collective-permute-done((f32[10,64]{0,1:T(8,128)S(1)}, f32[10,64]{0,1:T(8,128)S(1)}, u32[]{:S(2)}, u32[]{:S(2)}) %collective-permute-start.1) | collective-permute-done | bytes 2592 | tf_op jit(solution)/shard_map/ppermute | solution.py:14
  121.9 0.8 fusion.17
  122.7 62.3 %all-reduce.13.cloned.1.call-done = (f32[3,64,128]{2,1,0:T(8,128)}, f32[16,64,512]{2,1,0:T(8,128)}) async-done(((f32[3,64,128]{2,1,0:T(8,128)}, f32[16,64,512]{2,1,0:T(8,128)}), (f32[3,64,128]{2,1,0:T(8,128)}, f32[16,64,512]{2,1,0:T(8,128)})) %all-reduce.13.cloned.1.call-update) | async-done | bytes 2195472 | tf_op jit(solution)/shard_map/psum | solution.py:86
  185.0 1.5 broadcast_multiply_fusion.1
  186.5 3.2 %broadcast_multiply_fusion = f32[16,64,512]{2,1,0:T(8,128)} fusion(f32[16,64,512]{2,1,0:T(8,128)} %get-tuple-element.5), kind=kLoop, calls=%fused_computation.10 | loop fusion | flops 524288 | bytes 4194304 | tf_op jit(solution)/shard_map/mul | solution.py:96
  (2 shorter events, 0.1 us)
Async XLA Ops:
  7.2 12.0 %copy-start = (bf16[1,128,512]{2,1,0:T(8,128)(2,1)S(1)}, bf16[1,128,512]{2,1,0:T(8,128)(2,1)}, u32[]{:S(2)}) copy-start(bf16[1,128,512]{2,1,0:T(8,128)(2,1)} %param.9) | copy-start | bytes 393220
  7.2 10.6 %copy-start.3 = (bf16[3,64,128]{2,1,0:T(8,128)(2,1)S(1)}, bf16[3,64,128]{2,1,0:T(8,128)(2,1)}, u32[]{:S(2)}) copy-start(bf16[3,64,128]{2,1,0:T(8,128)(2,1)} %param.6) | copy-start | bytes 147460
  7.2 11.8 %copy-start.1 = (bf16[16,64,512]{2,1,0:T(8,128)(2,1)S(1)}, bf16[16,64,512]{2,1,0:T(8,128)(2,1)}, u32[]{:S(2)}) copy-start(bf16[16,64,512]{2,1,0:T(8,128)(2,1)} %param.8) | copy-start | bytes 3145732
  7.2 30.7 %all-gather.3.cloned.1.call-start = ((), (), s32[]{:S(2)}) async-start(), calls=%async_computation.1 | async-start | bytes 1320960 | tf_op jit(solution)/shard_map/all_gather | solution.py:54
  8.1 6.4 %collective-permute-start = (bf16[10,64]{0,1:T(8,128)(2,1)S(1)}, bf16[10,64]{0,1:T(8,128)(2,1)S(1)}, u32[]{:S(2)}, u32[]{:S(2)}) collective-permute-start(bf16[10,64]{0,1:T(8,128)(2,1)S(1)} %slice_bitcast_fusion), channel_id=1, source_target_pairs={{0,4},{4,8},{8,12},{1,5},{5,9},{9,13},{2,6},{6,10},{10,14},{3,7},{... | collective-permute-start | bytes 3848 | tf_op jit(solution)/shard_map/ppermute | solution.py:14
  19.0 54.1 %all-reduce.11.cloned.1.call-start = ((), (), s32[]{:S(2)}) async-start(), calls=%async_computation | async-start | bytes 528384 | tf_op jit(solution)/shard_map/psum | solution.py:75
  19.8 19.6 %copy-start.2 = (bf16[1,1024,64]{1,2,0:T(8,128)(2,1)S(1)}, bf16[1,1024,64]{1,2,0:T(8,128)(2,1)}, u32[]{:S(2)}) copy-start(bf16[1,1024,64]{1,2,0:T(8,128)(2,1)} %param.5) | copy-start | bytes 393220
  19.8 19.6 %copy-start.4 = (bf16[128,64]{0,1:T(8,128)(2,1)S(1)}, bf16[128,64]{0,1:T(8,128)(2,1)}, u32[]{:S(2)}) copy-start(bf16[128,64]{0,1:T(8,128)(2,1)} %param.7) | copy-start | bytes 49156
  41.7 143.3 %all-reduce.13.cloned.1.call-start = ((), (), s32[]{:S(2)}) async-start(), calls=%async_computation.2 | async-start | bytes 4390912 | tf_op jit(solution)/shard_map/psum | solution.py:86
  116.1 5.8 %collective-permute-start.1 = (f32[10,64]{0,1:T(8,128)S(1)}, f32[10,64]{0,1:T(8,128)S(1)}, u32[]{:S(2)}, u32[]{:S(2)}) collective-permute-start(f32[10,64]{0,1:T(8,128)S(1)} %slice.82), channel_id=1, source_target_pairs={{4,0},{8,4},{12,8},{5,1},{9,5},{13,9},{6,2},{10,6},{14,10},{7,3},{... | collective-permute-start | bytes 7688 | tf_op jit(solution)/shard_map/ppermute | solution.py:14
Sparse Core Ops, SparseCore 0:
  19.1 18.7 all-gather.2
  41.9 31.2 all-reduce.10
  77.5 107.4 all-reduce.12
